TPU v7x, 128 devices: a whole 4x4x4 slice. The times are simulated.
128 devices in a mesh: rows: 4 (over x_lo, core), hidden: 32 (over x_hi, z, y).
Axes of the slice: x: 4 (x_hi: 2, x_lo: 2; x = x_hi * 2 + x_lo), y: 4, z: 4, core: 2. Of those that a mesh axis runs over, the one named last changes fastest.
Arguments:
- resid_stream: bfloat16 [1024, 3584], P('rows'), may hold values from -6 to 6
- pre_gain: float32 [3584], replicated, may hold values from -0.5 to 0.5
- w_gate: bfloat16 [3584, 14336], P(None, 'hidden'), may hold values from -0.09375 to 0.09375
- w_up: bfloat16 [3584, 14336], P(None, 'hidden'), may hold values from -0.09375 to 0.09375
- w_down: bfloat16 [14336, 3584], P('hidden'), may hold values from -0.09375 to 0.09375
- w_enc: bfloat16 [3584, 32768], P(None, ('rows', 'hidden')), may hold values from -0.09375 to 0.09375
- b_enc: bfloat16 [32768], P(('rows', 'hidden')), may hold values from -3 to 3
- w_dec: bfloat16 [32768, 3584], P(('rows', 'hidden')), may hold values from -0.03125 to 0.03125
- b_dec: float32 [3584], replicated, may hold values from -3 to 3
Outputs:
- enc_grad: float32 [3584, 32768], P(None, ('rows', 'hidden'))
- dec_grad: float32 [32768, 3584], P(('rows', 'hidden'))
All inputs are finite; a program needn't handle non-finite values.
Results may differ from a plain program's by a relative error of at most 0.0062.
Values may be sent and summed in bfloat16 or wider, within the bound.
No kernel may reach another device: no remote copies, remote signals or barrier semaphores. Data moves between devices by JAX's collectives and lax.ppermute only.
A program may use at most 128 MiB of HBM per device.

v0:
```python
import math

import jax
import jax.numpy as jnp
from jax import lax
from jax.sharding import Mesh
from jax.sharding import PartitionSpec as P


F32 = jnp.float32
BF16 = jnp.bfloat16
ROWS = ("xl", "c")
HIDDEN = ("xh", "z", "y")
ALL = ("xl", "c", "xh", "z", "y")
SHIFTS = ((1, 1, 0), (0, 0, 1))


def scale_of(values):
    values = values.astype(F32)
    return lax.rsqrt(jnp.mean(values * values, axis=-1, keepdims=True) + 1e-06)


def normed(values, scale, pre_gain):
    return (values.astype(F32) * scale * (1.0 + pre_gain)).astype(BF16)


def dot(left, right):
    return jnp.dot(left, right, preferred_element_type=F32)


def contract_first(left, right):
    return lax.dot_general(left, right, (((0,), (0,)), ((), ())), preferred_element_type=F32)


def contract_last(left, right):
    return lax.dot_general(left, right, (((1,), (1,)), ((), ())), preferred_element_type=F32)


def index_of(x, core, z, y):
    return (((x % 2) * 2 + core) * 2 + x // 2) * 16 + z * 4 + y


def devices():
    return [(x, core, z, y) for x in range(4) for core in range(2) for z in range(4) for y in range(4)]


def far_rows(values):
    pairs = [
        (index_of(x, core, z, y), index_of((x + 1 - 2 * core) % 4, core, z, y))
        for x, core, z, y in devices()
    ]
    return lax.ppermute(values, ALL, pairs)


def cube_groups(outer):
    groups = {}
    for x, core, z, y in devices():
        moved = [(v + step) % 4 for v, step in zip((x, z, y), SHIFTS[core])]
        cube = tuple(v // 2 for v in moved)
        place = tuple(min(v, 3 - v) for v in moved)
        key, order = (cube, place) if outer else (place, cube)
        groups.setdefault((core, key), []).append((order, index_of(x, core, z, y)))
    return [[device for _, device in sorted(members)] for _, members in sorted(groups.items())]


def exchange(values, outer):
    return lax.all_to_all(values, ALL, 0, 0, axis_index_groups=cube_groups(outer), tiled=True)


def other_core(values):
    return lax.ppermute(values, "c", [(0, 1), (1, 0)])


def added(blocks):
    total = blocks[0].astype(F32)
    for block in blocks[1:]:
        total = total + block.astype(F32)
    return total


def swap_if(flag, values):
    half = values.shape[0] // 2
    return jnp.where(flag, jnp.concatenate([values[half:], values[:half]], axis=0), values)


def on_device(resid_stream, pre_gain, w_gate, w_up, w_down, w_enc, b_enc, w_dec, b_dec):
    rows, width = resid_stream.shape
    factor = 1.0 / math.sqrt(rows * lax.axis_size(ROWS))
    odd = lax.axis_index("xl") == 1

    far_resid = far_rows(resid_stream)
    enc_2 = jnp.concatenate([w_enc, other_core(w_enc)], axis=1)
    dec_2 = jnp.concatenate([w_dec, other_core(w_dec)], axis=0)
    bias_2 = jnp.concatenate([b_enc, other_core(b_enc)], axis=0).astype(F32)

    scale = scale_of(resid_stream)
    far_scale = far_rows(scale)
    near = normed(resid_stream, scale, pre_gain)
    hidden_units = (jax.nn.gelu(dot(near, w_gate), approximate=True) * dot(near, w_up)).astype(BF16)
    mine = swap_if(odd, jnp.concatenate([hidden_units, jnp.zeros_like(hidden_units)], axis=0))
    target = dot(mine, w_down)
    near_act = jnp.maximum(dot(near, enc_2) + bias_2, 0.0)
    far_resid, target, near_act, dec_2 = lax.optimization_barrier((far_resid, target, near_act, dec_2))
    far = normed(far_resid, far_scale, pre_gain)
    far_act = jnp.maximum(dot(far, enc_2) + bias_2, 0.0)
    rectified = swap_if(odd, jnp.concatenate([near_act, far_act], axis=0))
    latent = (rectified * rectified).astype(BF16)
    part = (dot(latent, dec_2) - target).astype(BF16)

    arrived = exchange(part.reshape(8, part.shape[0] // 8, width), True)
    summed = added(arrived).astype(BF16)
    arrived = exchange(summed.reshape(8, summed.shape[0] // 8, width), False)
    misfit = (added(arrived) + b_dec).astype(BF16)
    for outer in (False, True):
        spread = jnp.broadcast_to(misfit[None], (8,) + misfit.shape)
        misfit = exchange(spread, outer).reshape(8 * misfit.shape[0], width)
    misfit_all = misfit

    own = w_dec.shape[0]
    dec_out = contract_first(latent[:, own:], misfit_all).astype(BF16)
    dec_sent = other_core(dec_out)
    misfit_all, dec_out = lax.optimization_barrier((misfit_all, dec_out))
    slope = (contract_last(misfit_all, dec_2) * 2.0 * rectified).astype(BF16)
    slope = swap_if(odd, slope)
    normal_in = jnp.concatenate([near, far], axis=0)
    enc_out = contract_first(normal_in, slope[:, own:]).astype(BF16)
    enc_sent = other_core(enc_out)
    latent, slope, enc_out = lax.optimization_barrier((latent, slope, enc_out))
    dec_sum = (contract_first(latent[:, :own], misfit_all) + dec_sent.astype(F32)) * factor
    enc_sum = (contract_first(normal_in, slope[:, :own]) + enc_sent.astype(F32)) * factor
    return enc_sum, dec_sum


def solution(mesh):
    fine = Mesh(mesh.devices.reshape(2, 2, 2, 4, 4), ("xl", "c", "xh", "z", "y"))
    return jax.shard_map(
        on_device,
        mesh=fine,
        in_specs=(
            P(ROWS, None),
            P(),
            P(None, HIDDEN),
            P(None, HIDDEN),
            P(HIDDEN, None),
            P(None, ROWS + HIDDEN),
            P(ROWS + HIDDEN),
            P(ROWS + HIDDEN, None),
            P(),
        ),
        out_specs=(P(None, ROWS + HIDDEN), P(ROWS + HIDDEN, None)),
        check_vma=False,
    )
```

profile of v0, /device:TPU:1, one launch (start us, length us, event | category | flops | bytes accessed | tf_op | source)
XLA Modules:
  0.0 132.6 jit_solution(15994054099644494227)
XLA Ops:
  0.6 1.5 %collective-permute-start.2 = (bf16[256]{0:T(256)(128)(2,1)}, bf16[256]{0:T(256)(128)(2,1)S(1)}, u32[]{:S(2)}, u32[]{:S(2)}) collective-permute-start(bf16[256]{0:T(256)(128)(2,1)} %param.15), channel_id=1, source_target_pairs={{0,32},{32,0},{1,33},{33,1},{2,34},{34,2},{3,35},{35,3},{4,36},{36... | collective-permute-start | bytes 1544 | tf_op jit(solution)/shard_map/ppermute | solution.py:71
  2.1 2.6 %collective-permute-start = (bf16[256,3584]{1,0:T(8,128)(2,1)}, bf16[256,3584]{1,0:T(8,128)(2,1)}, u32[]{:S(2)}, u32[]{:S(2)}) collective-permute-start(bf16[256,3584]{1,0:T(8,128)(2,1)} %param.9), channel_id=1, source_target_pairs={{0,64},{1,65},{2,66},{3,67},{4,68},{5,69},{6,70},{7,71},{8,72},{9,... | collective-permute-start | bytes 5505032 | tf_op jit(solution)/shard_map/ppermute | solution.py:52
  4.7 2.0 %fusion = f32[256]{0:T(256)S(1)} fusion(bf16[256,3584]{1,0:T(8,128)(2,1)} %param.9), kind=kLoop, calls=%fused_computation.5 | loop fusion | flops 2752256 | bytes 1836032 | tf_op jit(solution)/shard_map/reduce_sum | solution.py:20
  8.5 3.2 %fusion.2 = bf16[256,3584]{1,0:T(8,128)(2,1)} fusion(bf16[256,3584]{1,0:T(8,128)(2,1)} %param.9, f32[3584]{0:T(1024)S(1)} %broadcast_add_fusion, f32[256]{0:T(256)S(1)} %add_rsqrt_fusion), kind=kLoop, calls=%fused_computation.7 | loop fusion | flops 3670016 | bytes 3685376 | tf_op jit(solution)/shard_map/convert_element_type | solution.py:24
  11.8 3.6 %fusion.34 = f32[256,448]{0,1:T(8,128)S(1)} fusion(bf16[256,3584]{1,0:T(8,128)(2,1)} %fusion.2, bf16[3584,448]{0,1:T(8,128)(2,1)} %param.11), kind=kOutput, calls=%fused_computation.57 | convolution fusion | flops 822083584 | bytes 5505024 | tf_op jit(solution)/shard_map/dot_general | solution.py:28
  15.7 1.0 fusion.8
  17.4 2.1 %fusion.17 = f32[512,3584]{1,0:T(8,128)S(1)} fusion(bf16[448,3584]{1,0:T(8,128)(2,1)S(1)} %copy-done, bf16[256,448]{0,1:T(8,128)(2,1)S(1)} %fusion.8, pred[]{:T(512)S(6)} %eq.3), kind=kOutput, calls=%fused_computation.36 | convolution fusion | flops 1644396544 | bytes 10780673 | tf_op jit(solution)/shard_map/dot_general | solution.py:28
  19.6 1.8 %constant_dynamic-update-slice_fusion = bf16[3584,512]{1,0:T(8,128)(2,1)S(1)} fusion(bf16[3584,512]{1,0:T(8,128)(2,1)S(1)} %constant_dynamic-update-slice_fusion.1, bf16[3584,256]{1,0:T(8,128)(2,1)} %collective-permute-done.1), kind=kLoop, calls=%fused_computation.49 | loop fusion | bytes 3670016 | tf_op jit(solution)/shard_map/concatenate | solution.py:92
  21.6 1.7 %pad_maximum_fusion = bf16[512,3584]{1,0:T(8,128)(2,1)S(1)} fusion(bf16[256,3584]{1,0:T(8,128)(2,1)} %collective-permute-done.3, bf16[256,3584]{1,0:T(8,128)(2,1)S(1)} %copy-done.2), kind=kLoop, calls=%fused_computation.8 | loop fusion | flops 7340032 | bytes 7340032 | tf_op jit(solution)/shard_map/concatenate | solution.py:93
  23.3 1.1 fusion.7
  25.2 2.0 %multiply_convert_fusion = bf16[256,3584]{1,0:T(8,128)(2,1)S(1)} fusion(bf16[256,3584]{1,0:T(8,128)(2,1)} %collective-permute-done, f32[256]{0:T(256)S(1)} %bitcast.30, f32[3584]{0:T(1024)S(1)} %broadcast_add_fusion), kind=kLoop, calls=%fused_computation.12 | loop fusion | flops 3670016 | bytes 3685376 | tf_op jit(solution)/shard_map/convert_element_type | solution.py:24
  27.2 1.1 fusion.6
  28.5 2.1 %subtract_convert_fusion = bf16[512,3584]{1,0:T(8,128)(2,1)S(1)} fusion(f32[512,3584]{1,0:T(8,128)S(1)} %fusion.17, bf16[512,512]{1,0:T(8,128)(2,1)S(1)} %multiply_convert_fusion.1, bf16[512,3584]{1,0:T(8,128)(2,1)S(1)} %pad_maximum_fusion), kind=kOutput, calls=%fused_computation | convolution fusion | flops 1882718208 | bytes 15204352 | tf_op jit(solution)/shard_map/dot_general | solution.py:28
  30.6 28.6 %all_to_all.20 = bf16[8,64,3584]{2,1,0:T(8,128)(2,1)S(1)} all-to-all(bf16[8,64,3584]{2,1,0:T(8,128)(2,1)S(1)} %bitcast.27), channel_id=1, replica_groups={{92,93,80,81,12,13,0,1},{95,94,83,82,15,14,3,2},{88,89,84,85,8,9,4,5},{..., dimensions={0} | all-to-all | bytes 7340032 | tf_op jit(solution)/shard_map/all_to_all | solution.py:67
  59.7 15.8 %all_to_all.21 = bf16[8,8,3584]{2,1,0:T(8,128)(2,1)S(1)} all-to-all(bf16[8,8,3584]{2,1,0:T(8,128)(2,1)S(1)} %fusion.16), channel_id=1, replica_groups={{92,95,88,91,28,31,24,27},{93,94,89,90,29,30,25,26},{80,83,84,87,16,19,..., dimensions={0} | all-to-all | bytes 917504 | tf_op jit(solution)/shard_map/all_to_all | solution.py:67
  75.6 11.4 %all_to_all.22 = bf16[8,8,3584]{2,1,0:T(8,128)(2,1)S(1)} all-to-all(bf16[8,8,3584]{2,1,0:T(8,128)(2,1)S(1)} %broadcast_in_dim.9), channel_id=1, replica_groups={{92,95,88,91,28,31,24,27},{93,94,89,90,29,30,25,26},{80,83,84,87,16,19,..., dimensions={0} | all-to-all | bytes 917504 | tf_op jit(solution)/shard_map/all_to_all | solution.py:67
  87.3 27.4 %all_to_all.23 = bf16[8,64,3584]{2,1,0:T(8,128)(2,1)S(1)} all-to-all(bf16[8,64,3584]{2,1,0:T(8,128)(2,1)S(1)} %broadcast_in_dim.11), channel_id=1, replica_groups={{92,93,80,81,12,13,0,1},{95,94,83,82,15,14,3,2},{88,89,84,85,8,9,4,5},{..., dimensions={0} | all-to-all | bytes 7340032 | tf_op jit(solution)/shard_map/all_to_all | solution.py:67
  114.8 1.2 convolution_convert_fusion.1
  115.9 2.1 %fusion.5 = bf16[512,512]{1,0:T(8,128)(2,1)S(1)} fusion(bf16[512,3584]{1,0:T(8,128)(2,1)S(1)} %bitcast.25, bf16[512,3584]{1,0:T(8,128)(2,1)S(1)} %pad_maximum_fusion, f32[256,512]{1,0:T(8,128)S(1)} %fusion.6, f32[256,512]{1,0:T(8,128)S(1)} %fusion.7, pred[]{:T(512)S(6)} %eq.3), kind=kOutput, calls=%fused_computation.16 | convolution fusion | flops 1880621056 | bytes 8912897 | tf_op jit(solution)/shard_map/dot_general | solution.py:36
  118.2 1.2 convolution_convert_fusion
  119.4 3.7 %collective-permute-start.5 = (bf16[3584,256]{1,0:T(8,128)(2,1)S(1)}, bf16[3584,256]{1,0:T(8,128)(2,1)S(1)}, u32[]{:S(2)}, u32[]{:S(2)}) collective-permute-start(bf16[3584,256]{1,0:T(8,128)(2,1)S(1)} %convolution_convert_fusion), channel_id=1, source_target_pairs={{0,32},{32,0},{1,33},{33,1},{2,34},{34,2},{3,35},{35,3},{4,36},{36... | collective-permute-start | bytes 5505032 | tf_op jit(solution)/shard_map/ppermute | solution.py:71
  123.2 3.3 %collective-permute-done.5 = bf16[3584,256]{1,0:T(8,128)(2,1)S(1)} collective-permute-done((bf16[3584,256]{1,0:T(8,128)(2,1)S(1)}, bf16[3584,256]{1,0:T(8,128)(2,1)S(1)}, u32[]{:S(2)}, u32[]{:S(2)}) %collective-permute-start.5) | collective-permute-done | bytes 1835040 | tf_op jit(solution)/shard_map/ppermute | solution.py:71
  126.5 3.0 %add_multiply_fusion.1 = f32[3584,256]{1,0:T(8,128)} fusion(bf16[3584,256]{1,0:T(8,128)(2,1)S(1)} %collective-permute-done.5, bf16[256,3584]{1,0:T(8,128)(2,1)S(1)} %multiply_convert_fusion, bf16[256,3584]{1,0:T(8,128)(2,1)S(1)} %copy-done.4, bf16[512,512]{1,0:T(8,128)(2,1)S(1)} %maximum_select_fusion.1), kind=kOutput, calls=%fused_computation.11 | convolution fusion | flops 949616640 | bytes 9437184 | tf_op jit(solution)/shard_map/dot_general | solution.py:32
  129.5 3.0 %add_multiply_fusion = f32[256,3584]{1,0:T(8,128)} fusion(bf16[256,3584]{1,0:T(8,128)(2,1)S(1)} %collective-permute-done.6, bf16[512,3584]{1,0:T(8,128)(2,1)S(1)} %bitcast.26, bf16[512,512]{1,0:T(8,128)(2,1)S(1)} %multiply_convert_fusion.1), kind=kOutput, calls=%fused_computation.10 | convolution fusion | flops 942276608 | bytes 9437184 | tf_op jit(solution)/shard_map/dot_general | solution.py:32
  (37 shorter events, 5.1 us)
Async XLA Ops:
  0.6 16.8 %copy-start = (bf16[448,3584]{1,0:T(8,128)(2,1)S(1)}, bf16[448,3584]{1,0:T(8,128)(2,1)}, u32[]{:S(2)}) copy-start(bf16[448,3584]{1,0:T(8,128)(2,1)} %param.13) | copy-start | bytes 9633796
  0.6 18.9 %collective-permute-start.2 = (bf16[256]{0:T(256)(128)(2,1)}, bf16[256]{0:T(256)(128)(2,1)S(1)}, u32[]{:S(2)}, u32[]{:S(2)}) collective-permute-start(bf16[256]{0:T(256)(128)(2,1)} %param.15), channel_id=1, source_target_pairs={{0,32},{32,0},{1,33},{33,1},{2,34},{34,2},{3,35},{35,3},{4,36},{36... | collective-permute-start | bytes 1544 | tf_op jit(solution)/shard_map/ppermute | solution.py:71
  2.1 23.1 %collective-permute-start = (bf16[256,3584]{1,0:T(8,128)(2,1)}, bf16[256,3584]{1,0:T(8,128)(2,1)}, u32[]{:S(2)}, u32[]{:S(2)}) collective-permute-start(bf16[256,3584]{1,0:T(8,128)(2,1)} %param.9), channel_id=1, source_target_pairs={{0,64},{1,65},{2,66},{3,67},{4,68},{5,69},{6,70},{7,71},{8,72},{9,... | collective-permute-start | bytes 5505032 | tf_op jit(solution)/shard_map/ppermute | solution.py:52
  6.7 18.5 %collective-permute-start.4 = (f32[256,1]{0,1:T(1,128)S(1)}, f32[256,1]{0,1:T(1,128)S(1)}, u32[]{:S(2)}, u32[]{:S(2)}) collective-permute-start(f32[256,1]{0,1:T(1,128)S(1)} %bitcast.29), channel_id=1, source_target_pairs={{0,64},{1,65},{2,66},{3,67},{4,68},{5,69},{6,70},{7,71},{8,72},{9,... | collective-permute-start | bytes 3080 | tf_op jit(solution)/shard_map/ppermute | solution.py:52
  7.3 12.3 %collective-permute-start.1 = (bf16[3584,256]{1,0:T(8,128)(2,1)}, bf16[3584,256]{1,0:T(8,128)(2,1)}, u32[]{:S(2)}, u32[]{:S(2)}) collective-permute-start(bf16[3584,256]{1,0:T(8,128)(2,1)} %param.14), channel_id=1, source_target_pairs={{0,32},{32,0},{1,33},{33,1},{2,34},{34,2},{3,35},{35,3},{4,36},{36... | collective-permute-start | bytes 5505032 | tf_op jit(solution)/shard_map/ppermute | solution.py:71
  7.3 14.0 %collective-permute-start.3 = (bf16[256,3584]{1,0:T(8,128)(2,1)}, bf16[256,3584]{1,0:T(8,128)(2,1)}, u32[]{:S(2)}, u32[]{:S(2)}) collective-permute-start(bf16[256,3584]{1,0:T(8,128)(2,1)} %param.16), channel_id=1, source_target_pairs={{0,32},{32,0},{1,33},{33,1},{2,34},{34,2},{3,35},{35,3},{4,36},{36... | collective-permute-start | bytes 5505032 | tf_op jit(solution)/shard_map/ppermute | solution.py:71
  11.8 3.6 %copy-start.4 = (bf16[256,3584]{1,0:T(8,128)(2,1)S(1)}, bf16[256,3584]{1,0:T(8,128)(2,1)}, u32[]{:S(2)}) copy-start(bf16[256,3584]{1,0:T(8,128)(2,1)} %fusion.2) | copy-start | bytes 5505028
  11.8 4.0 %copy-start.7 = (bf16[3584,448]{0,1:T(8,128)(2,1)S(1)}, bf16[3584,448]{0,1:T(8,128)(2,1)}, u32[]{:S(2)}) copy-start(bf16[3584,448]{0,1:T(8,128)(2,1)} %param.12) | copy-start | bytes 9633796
  15.7 1.5 %copy-start.3 = (bf16[3584,256]{1,0:T(8,128)(2,1)S(1)}, bf16[3584,256]{1,0:T(8,128)(2,1)}, u32[]{:S(2)}) copy-start(bf16[3584,256]{1,0:T(8,128)(2,1)} %param.14) | copy-start | bytes 5505028
  17.4 2.2 %copy-start.6 = (bf16[256]{0:T(256)(128)(2,1)S(1)}, bf16[256]{0:T(256)(128)(2,1)}, u32[]{:S(2)}) copy-start(bf16[256]{0:T(256)(128)(2,1)} %param.15) | copy-start | bytes 1540
  19.5 2.1 %copy-start.2 = (bf16[256,3584]{1,0:T(8,128)(2,1)S(1)}, bf16[256,3584]{1,0:T(8,128)(2,1)}, u32[]{:S(2)}) copy-start(bf16[256,3584]{1,0:T(8,128)(2,1)} %param.16) | copy-start | bytes 5505028
  59.2 16.3 %copy-start.5 = (f32[3584]{0:T(1024)S(1)}, f32[3584]{0:T(1024)}, u32[]{:S(2)}) copy-start(f32[3584]{0:T(1024)} %param.17) | copy-start | bytes 43012
  119.4 7.1 %collective-permute-start.5 = (bf16[3584,256]{1,0:T(8,128)(2,1)S(1)}, bf16[3584,256]{1,0:T(8,128)(2,1)S(1)}, u32[]{:S(2)}, u32[]{:S(2)}) collective-permute-start(bf16[3584,256]{1,0:T(8,128)(2,1)S(1)} %convolution_convert_fusion), channel_id=1, source_target_pairs={{0,32},{32,0},{1,33},{33,1},{2,34},{34,2},{3,35},{35,3},{4,36},{36... | collective-permute-start | bytes 5505032 | tf_op jit(solution)/shard_map/ppermute | solution.py:71
  123.1 6.4 %collective-permute-start.6 = (bf16[256,3584]{1,0:T(8,128)(2,1)S(1)}, bf16[256,3584]{1,0:T(8,128)(2,1)S(1)}, u32[]{:S(2)}, u32[]{:S(2)}) collective-permute-start(bf16[256,3584]{1,0:T(8,128)(2,1)S(1)} %convolution_convert_fusion.1), channel_id=1, source_target_pairs={{0,32},{32,0},{1,33},{33,1},{2,34},{34,2},{3,35},{35,3},{4,36},{36... | collective-permute-start | bytes 5505032 | tf_op jit(solution)/shard_map/ppermute | solution.py:71
  126.5 6.1 %copy-start.1 = (bf16[448,3584]{1,0:T(8,128)(2,1)S(1)}, bf16[448,3584]{1,0:T(8,128)(2,1)}, u32[]{:S(2)}) copy-start(bf16[448,3584]{1,0:T(8,128)(2,1)} %param.13) | copy-start | bytes 9633796
where the time goes:
time: 133 us
  blocking collectives  83.3 us (63%)
  matrix products  21.6 us (16%)
  other arithmetic  10.5 us (8%)
  starting transfers between devices  8.99 us (7%)
  waiting for transfers between devices  4.06 us (3%)
  local copies, waits for them, and re-layouts  3.3 us (2%)
    all_to_all x4, blocking collectives, exchange(): lax.all_to_all(values, ALL, 0, 0, axis_index_groups=cube_groups(outer), t...  83.3 us
    dot_general x6, matrix products, dot(): return jnp.dot(left, right, preferred_element_type=F32)  11.1 us
    dot_general x4, matrix products, contract_first(): lax.dot_general(left, right, (((0,), (0,)), ((), ())), preferred_element_...  8.39 us
    ppermute x5, starting transfers between devices, other_core(): return lax.ppermute(values, 'c', [(0, 1), (1, 0)])  5.79 us
    convert_element_type x2, other arithmetic, normed(): return (values.astype(F32) * scale * (1.0 + pre_gain)).astype(BF16)  5.24 us
    ppermute x5, waiting for transfers between devices, other_core(): return lax.ppermute(values, 'c', [(0, 1), (1, 0)])  3.33 us
    ppermute x2, starting transfers between devices, far_rows(): return lax.ppermute(values, ALL, pairs)  3.21 us
  transfers between devices with their start and end apart: 7, of which 2 were waited for; matrix products, arithmetic and copies ran while one was open for 15% of the time, Pallas kernels for 0%

commit v1 on v0

--- a/solution.py
+++ b/solution.py
@@ -12,7 +12,6 @@
 ROWS = ("xl", "c")
 HIDDEN = ("xh", "z", "y")
 ALL = ("xl", "c", "xh", "z", "y")
-SHIFTS = ((1, 1, 0), (0, 0, 1))
 
 
 def scale_of(values):
@@ -52,19 +51,19 @@
     return lax.ppermute(values, ALL, pairs)
 
 
-def cube_groups(outer):
+def groups_of_8(first):
     groups = {}
     for x, core, z, y in devices():
-        moved = [(v + step) % 4 for v, step in zip((x, z, y), SHIFTS[core])]
-        cube = tuple(v // 2 for v in moved)
-        place = tuple(min(v, 3 - v) for v in moved)
-        key, order = (cube, place) if outer else (place, cube)
+        line, across = (z, x) if core == 0 else (x, z)
+        turned = (y + 1 - core) % 4
+        group, place = (across, turned // 2), (line, min(turned, 3 - turned))
+        key, order = (group, place) if first else (place, group)
         groups.setdefault((core, key), []).append((order, index_of(x, core, z, y)))
     return [[device for _, device in sorted(members)] for _, members in sorted(groups.items())]
 
 
-def exchange(values, outer):
-    return lax.all_to_all(values, ALL, 0, 0, axis_index_groups=cube_groups(outer), tiled=True)
+def exchange(values, first):
+    return lax.all_to_all(values, ALL, 0, 0, axis_index_groups=groups_of_8(first), tiled=True)
 
 
 def other_core(values):
@@ -91,7 +90,8 @@
     far_resid = far_rows(resid_stream)
     enc_2 = jnp.concatenate([w_enc, other_core(w_enc)], axis=1)
     dec_2 = jnp.concatenate([w_dec, other_core(w_dec)], axis=0)
-    bias_2 = jnp.concatenate([b_enc, other_core(b_enc)], axis=0).astype(F32)
+    far_bias = other_core(b_enc)
+    bias_2 = jnp.concatenate([b_enc, far_bias], axis=0).astype(F32)
 
     scale = scale_of(resid_stream)
     far_scale = far_rows(scale)
@@ -111,9 +111,9 @@
     summed = added(arrived).astype(BF16)
     arrived = exchange(summed.reshape(8, summed.shape[0] // 8, width), False)
     misfit = (added(arrived) + b_dec).astype(BF16)
-    for outer in (False, True):
+    for first in (False, True):
         spread = jnp.broadcast_to(misfit[None], (8,) + misfit.shape)
-        misfit = exchange(spread, outer).reshape(8 * misfit.shape[0], width)
+        misfit = exchange(spread, first).reshape(8 * misfit.shape[0], width)
     misfit_all = misfit
 
     own = w_dec.shape[0]

time: 133 us -> 132 us (level)
  transfers between devices with their start and end apart: 7 -> 7, of which waited for: 2 -> 2; matrix products, arithmetic and copies ran while one was open for 15% -> 16% of each run, Pallas kernels for 0% -> 0%
where the time goes in v1:
time: 132 us; the launch traced here: 131 us
  blocking collectives  82.3 us (62%)
  matrix products  21.6 us (16%)
  other arithmetic  10.5 us (8%)
  starting transfers between devices  8.55 us (6%)
  waiting for transfers between devices  4.06 us (3%)
  local copies, waits for them, and re-layouts  3.3 us (2%)
    all_to_all x4, blocking collectives, exchange(): lax.all_to_all(values, ALL, 0, 0, axis_index_groups=groups_of_8(first), t...  82.3 us
    dot_general x6, matrix products, dot(): return jnp.dot(left, right, preferred_element_type=F32)  11.1 us
    dot_general x4, matrix products, contract_first(): lax.dot_general(left, right, (((0,), (0,)), ((), ())), preferred_element_...  8.39 us
    ppermute x5, starting transfers between devices, other_core(): return lax.ppermute(values, 'c', [(0, 1), (1, 0)])  5.34 us
    convert_element_type x2, other arithmetic, normed(): return (values.astype(F32) * scale * (1.0 + pre_gain)).astype(BF16)  5.24 us
    ppermute x5, waiting for transfers between devices, other_core(): return lax.ppermute(values, 'c', [(0, 1), (1, 0)])  3.33 us
    ppermute x2, starting transfers between devices, far_rows(): return lax.ppermute(values, ALL, pairs)  3.21 us
  transfers between devices with their start and end apart: 7, of which 2 were waited for; matrix products, arithmetic and copies ran while one was open for 16% of the time, Pallas kernels for 0%

profile of v1, /device:TPU:1, one launch (start us, length us, event | category | flops | bytes accessed | tf_op | source)
XLA Modules:
  0.0 131.2 jit_solution(4924201953823187121)
XLA Ops:
  0.6 1.5 %collective-permute-start.2 = (bf16[256]{0:T(256)(128)(2,1)}, bf16[256]{0:T(256)(128)(2,1)S(1)}, u32[]{:S(2)}, u32[]{:S(2)}) collective-permute-start(bf16[256]{0:T(256)(128)(2,1)} %param.15), channel_id=1, source_target_pairs={{0,32},{32,0},{1,33},{33,1},{2,34},{34,2},{3,35},{35,3},{4,36},{36... | collective-permute-start | bytes 1544 | tf_op jit(solution)/shard_map/ppermute | solution.py:70
  2.1 2.6 %collective-permute-start = (bf16[256,3584]{1,0:T(8,128)(2,1)}, bf16[256,3584]{1,0:T(8,128)(2,1)}, u32[]{:S(2)}, u32[]{:S(2)}) collective-permute-start(bf16[256,3584]{1,0:T(8,128)(2,1)} %param.9), channel_id=1, source_target_pairs={{0,64},{1,65},{2,66},{3,67},{4,68},{5,69},{6,70},{7,71},{8,72},{9,... | collective-permute-start | bytes 5505032 | tf_op jit(solution)/shard_map/ppermute | solution.py:51
  4.7 2.0 %fusion = f32[256]{0:T(256)S(1)} fusion(bf16[256,3584]{1,0:T(8,128)(2,1)} %param.9), kind=kLoop, calls=%fused_computation.5 | loop fusion | flops 2752256 | bytes 1836032 | tf_op jit(solution)/shard_map/reduce_sum | solution.py:19
  8.5 3.2 %fusion.2 = bf16[256,3584]{1,0:T(8,128)(2,1)} fusion(bf16[256,3584]{1,0:T(8,128)(2,1)} %param.9, f32[3584]{0:T(1024)S(1)} %broadcast_add_fusion, f32[256]{0:T(256)S(1)} %add_rsqrt_fusion), kind=kLoop, calls=%fused_computation.7 | loop fusion | flops 3670016 | bytes 3685376 | tf_op jit(solution)/shard_map/convert_element_type | solution.py:23
  11.8 3.6 %fusion.34 = f32[256,448]{0,1:T(8,128)S(1)} fusion(bf16[256,3584]{1,0:T(8,128)(2,1)} %fusion.2, bf16[3584,448]{0,1:T(8,128)(2,1)} %param.11), kind=kOutput, calls=%fused_computation.57 | convolution fusion | flops 822083584 | bytes 5505024 | tf_op jit(solution)/shard_map/dot_general | solution.py:27
  15.7 1.0 fusion.8
  17.4 2.1 %fusion.17 = f32[512,3584]{1,0:T(8,128)S(1)} fusion(bf16[448,3584]{1,0:T(8,128)(2,1)S(1)} %copy-done, bf16[256,448]{0,1:T(8,128)(2,1)S(1)} %fusion.8, pred[]{:T(512)S(6)} %eq.3), kind=kOutput, calls=%fused_computation.36 | convolution fusion | flops 1644396544 | bytes 10780673 | tf_op jit(solution)/shard_map/dot_general | solution.py:27
  19.6 1.8 %constant_dynamic-update-slice_fusion = bf16[3584,512]{1,0:T(8,128)(2,1)S(1)} fusion(bf16[3584,512]{1,0:T(8,128)(2,1)S(1)} %constant_dynamic-update-slice_fusion.1, bf16[3584,256]{1,0:T(8,128)(2,1)} %collective-permute-done.1), kind=kLoop, calls=%fused_computation.49 | loop fusion | bytes 3670016 | tf_op jit(solution)/shard_map/concatenate | solution.py:91
  21.6 1.7 %pad_maximum_fusion = bf16[512,3584]{1,0:T(8,128)(2,1)S(1)} fusion(bf16[256,3584]{1,0:T(8,128)(2,1)} %collective-permute-done.3, bf16[256,3584]{1,0:T(8,128)(2,1)S(1)} %copy-done.2), kind=kLoop, calls=%fused_computation.8 | loop fusion | flops 7340032 | bytes 7340032 | tf_op jit(solution)/shard_map/concatenate | solution.py:92
  23.3 1.1 fusion.7
  25.2 2.0 %multiply_convert_fusion = bf16[256,3584]{1,0:T(8,128)(2,1)S(1)} fusion(bf16[256,3584]{1,0:T(8,128)(2,1)} %collective-permute-done, f32[256]{0:T(256)S(1)} %bitcast.30, f32[3584]{0:T(1024)S(1)} %broadcast_add_fusion), kind=kLoop, calls=%fused_computation.12 | loop fusion | flops 3670016 | bytes 3685376 | tf_op jit(solution)/shard_map/convert_element_type | solution.py:23
  27.2 1.1 fusion.6
  28.5 2.1 %subtract_convert_fusion = bf16[512,3584]{1,0:T(8,128)(2,1)S(1)} fusion(f32[512,3584]{1,0:T(8,128)S(1)} %fusion.17, bf16[512,512]{1,0:T(8,128)(2,1)S(1)} %multiply_convert_fusion.1, bf16[512,3584]{1,0:T(8,128)(2,1)S(1)} %pad_maximum_fusion), kind=kOutput, calls=%fused_computation | convolution fusion | flops 1882718208 | bytes 15204352 | tf_op jit(solution)/shard_map/dot_general | solution.py:27
  30.6 29.5 %all_to_all.20 = bf16[8,64,3584]{2,1,0:T(8,128)(2,1)S(1)} all-to-all(bf16[8,64,3584]{2,1,0:T(8,128)(2,1)S(1)} %bitcast.27), channel_id=1, replica_groups={{3,0,7,4,11,8,15,12},{2,1,6,5,10,9,14,13},{67,64,71,68,75,72,79,76},{66..., dimensions={0} | all-to-all | bytes 7340032 | tf_op jit(solution)/shard_map/all_to_all | solution.py:66
  60.6 15.0 %all_to_all.21 = bf16[8,8,3584]{2,1,0:T(8,128)(2,1)S(1)} all-to-all(bf16[8,8,3584]{2,1,0:T(8,128)(2,1)S(1)} %fusion.16), channel_id=1, replica_groups={{3,2,67,66,19,18,83,82},{0,1,64,65,16,17,80,81},{7,6,71,70,23,22,87,86}..., dimensions={0} | all-to-all | bytes 917504 | tf_op jit(solution)/shard_map/all_to_all | solution.py:66
  75.7 10.9 %all_to_all.22 = bf16[8,8,3584]{2,1,0:T(8,128)(2,1)S(1)} all-to-all(bf16[8,8,3584]{2,1,0:T(8,128)(2,1)S(1)} %broadcast_in_dim.9), channel_id=1, replica_groups={{3,2,67,66,19,18,83,82},{0,1,64,65,16,17,80,81},{7,6,71,70,23,22,87,86}..., dimensions={0} | all-to-all | bytes 917504 | tf_op jit(solution)/shard_map/all_to_all | solution.py:66
  87.0 26.8 %all_to_all.23 = bf16[8,64,3584]{2,1,0:T(8,128)(2,1)S(1)} all-to-all(bf16[8,64,3584]{2,1,0:T(8,128)(2,1)S(1)} %broadcast_in_dim.11), channel_id=1, replica_groups={{3,0,7,4,11,8,15,12},{2,1,6,5,10,9,14,13},{67,64,71,68,75,72,79,76},{66..., dimensions={0} | all-to-all | bytes 7340032 | tf_op jit(solution)/shard_map/all_to_all | solution.py:66
  113.8 1.2 convolution_convert_fusion.1
  114.9 2.1 %fusion.5 = bf16[512,512]{1,0:T(8,128)(2,1)S(1)} fusion(bf16[512,3584]{1,0:T(8,128)(2,1)S(1)} %bitcast.25, bf16[512,3584]{1,0:T(8,128)(2,1)S(1)} %pad_maximum_fusion, f32[256,512]{1,0:T(8,128)S(1)} %fusion.6, f32[256,512]{1,0:T(8,128)S(1)} %fusion.7, pred[]{:T(512)S(6)} %eq.3), kind=kOutput, calls=%fused_computation.16 | convolution fusion | flops 1880621056 | bytes 8912897 | tf_op jit(solution)/shard_map/dot_general | solution.py:35
  117.2 1.2 convolution_convert_fusion
  118.4 3.3 %collective-permute-start.5 = (bf16[3584,256]{1,0:T(8,128)(2,1)S(1)}, bf16[3584,256]{1,0:T(8,128)(2,1)S(1)}, u32[]{:S(2)}, u32[]{:S(2)}) collective-permute-start(bf16[3584,256]{1,0:T(8,128)(2,1)S(1)} %convolution_convert_fusion), channel_id=1, source_target_pairs={{0,32},{32,0},{1,33},{33,1},{2,34},{34,2},{3,35},{35,3},{4,36},{36... | collective-permute-start | bytes 5505032 | tf_op jit(solution)/shard_map/ppermute | solution.py:70
  121.8 3.3 %collective-permute-done.5 = bf16[3584,256]{1,0:T(8,128)(2,1)S(1)} collective-permute-done((bf16[3584,256]{1,0:T(8,128)(2,1)S(1)}, bf16[3584,256]{1,0:T(8,128)(2,1)S(1)}, u32[]{:S(2)}, u32[]{:S(2)}) %collective-permute-start.5) | collective-permute-done | bytes 1835040 | tf_op jit(solution)/shard_map/ppermute | solution.py:70
  125.1 3.0 %add_multiply_fusion.1 = f32[3584,256]{1,0:T(8,128)} fusion(bf16[3584,256]{1,0:T(8,128)(2,1)S(1)} %collective-permute-done.5, bf16[256,3584]{1,0:T(8,128)(2,1)S(1)} %multiply_convert_fusion, bf16[256,3584]{1,0:T(8,128)(2,1)S(1)} %copy-done.4, bf16[512,512]{1,0:T(8,128)(2,1)S(1)} %maximum_select_fusion.1), kind=kOutput, calls=%fused_computation.11 | convolution fusion | flops 949616640 | bytes 9437184 | tf_op jit(solution)/shard_map/dot_general | solution.py:31
  128.1 3.0 %add_multiply_fusion = f32[256,3584]{1,0:T(8,128)} fusion(bf16[256,3584]{1,0:T(8,128)(2,1)S(1)} %collective-permute-done.6, bf16[512,3584]{1,0:T(8,128)(2,1)S(1)} %bitcast.26, bf16[512,512]{1,0:T(8,128)(2,1)S(1)} %multiply_convert_fusion.1), kind=kOutput, calls=%fused_computation.10 | convolution fusion | flops 942276608 | bytes 9437184 | tf_op jit(solution)/shard_map/dot_general | solution.py:31
  (37 shorter events, 5.1 us)
Async XLA Ops:
  0.6 16.8 %copy-start = (bf16[448,3584]{1,0:T(8,128)(2,1)S(1)}, bf16[448,3584]{1,0:T(8,128)(2,1)}, u32[]{:S(2)}) copy-start(bf16[448,3584]{1,0:T(8,128)(2,1)} %param.13) | copy-start | bytes 9633796
  0.6 18.9 %collective-permute-start.2 = (bf16[256]{0:T(256)(128)(2,1)}, bf16[256]{0:T(256)(128)(2,1)S(1)}, u32[]{:S(2)}, u32[]{:S(2)}) collective-permute-start(bf16[256]{0:T(256)(128)(2,1)} %param.15), channel_id=1, source_target_pairs={{0,32},{32,0},{1,33},{33,1},{2,34},{34,2},{3,35},{35,3},{4,36},{36... | collective-permute-start | bytes 1544 | tf_op jit(solution)/shard_map/ppermute | solution.py:70
  2.1 23.1 %collective-permute-start = (bf16[256,3584]{1,0:T(8,128)(2,1)}, bf16[256,3584]{1,0:T(8,128)(2,1)}, u32[]{:S(2)}, u32[]{:S(2)}) collective-permute-start(bf16[256,3584]{1,0:T(8,128)(2,1)} %param.9), channel_id=1, source_target_pairs={{0,64},{1,65},{2,66},{3,67},{4,68},{5,69},{6,70},{7,71},{8,72},{9,... | collective-permute-start | bytes 5505032 | tf_op jit(solution)/shard_map/ppermute | solution.py:51
  6.7 18.5 %collective-permute-start.4 = (f32[256,1]{0,1:T(1,128)S(1)}, f32[256,1]{0,1:T(1,128)S(1)}, u32[]{:S(2)}, u32[]{:S(2)}) collective-permute-start(f32[256,1]{0,1:T(1,128)S(1)} %bitcast.29), channel_id=1, source_target_pairs={{0,64},{1,65},{2,66},{3,67},{4,68},{5,69},{6,70},{7,71},{8,72},{9,... | collective-permute-start | bytes 3080 | tf_op jit(solution)/shard_map/ppermute | solution.py:51
  7.3 12.3 %collective-permute-start.1 = (bf16[3584,256]{1,0:T(8,128)(2,1)}, bf16[3584,256]{1,0:T(8,128)(2,1)}, u32[]{:S(2)}, u32[]{:S(2)}) collective-permute-start(bf16[3584,256]{1,0:T(8,128)(2,1)} %param.14), channel_id=1, source_target_pairs={{0,32},{32,0},{1,33},{33,1},{2,34},{34,2},{3,35},{35,3},{4,36},{36... | collective-permute-start | bytes 5505032 | tf_op jit(solution)/shard_map/ppermute | solution.py:70
  7.3 14.0 %collective-permute-start.3 = (bf16[256,3584]{1,0:T(8,128)(2,1)}, bf16[256,3584]{1,0:T(8,128)(2,1)}, u32[]{:S(2)}, u32[]{:S(2)}) collective-permute-start(bf16[256,3584]{1,0:T(8,128)(2,1)} %param.16), channel_id=1, source_target_pairs={{0,32},{32,0},{1,33},{33,1},{2,34},{34,2},{3,35},{35,3},{4,36},{36... | collective-permute-start | bytes 5505032 | tf_op jit(solution)/shard_map/ppermute | solution.py:70
  11.8 3.6 %copy-start.4 = (bf16[256,3584]{1,0:T(8,128)(2,1)S(1)}, bf16[256,3584]{1,0:T(8,128)(2,1)}, u32[]{:S(2)}) copy-start(bf16[256,3584]{1,0:T(8,128)(2,1)} %fusion.2) | copy-start | bytes 5505028
  11.8 4.0 %copy-start.7 = (bf16[3584,448]{0,1:T(8,128)(2,1)S(1)}, bf16[3584,448]{0,1:T(8,128)(2,1)}, u32[]{:S(2)}) copy-start(bf16[3584,448]{0,1:T(8,128)(2,1)} %param.12) | copy-start | bytes 9633796
  15.7 1.5 %copy-start.3 = (bf16[3584,256]{1,0:T(8,128)(2,1)S(1)}, bf16[3584,256]{1,0:T(8,128)(2,1)}, u32[]{:S(2)}) copy-start(bf16[3584,256]{1,0:T(8,128)(2,1)} %param.14) | copy-start | bytes 5505028
  17.4 2.2 %copy-start.6 = (bf16[256]{0:T(256)(128)(2,1)S(1)}, bf16[256]{0:T(256)(128)(2,1)}, u32[]{:S(2)}) copy-start(bf16[256]{0:T(256)(128)(2,1)} %param.15) | copy-start | bytes 1540
  19.5 2.1 %copy-start.2 = (bf16[256,3584]{1,0:T(8,128)(2,1)S(1)}, bf16[256,3584]{1,0:T(8,128)(2,1)}, u32[]{:S(2)}) copy-start(bf16[256,3584]{1,0:T(8,128)(2,1)} %param.16) | copy-start | bytes 5505028
  60.1 15.5 %copy-start.5 = (f32[3584]{0:T(1024)S(1)}, f32[3584]{0:T(1024)}, u32[]{:S(2)}) copy-start(f32[3584]{0:T(1024)} %param.17) | copy-start | bytes 43012
  118.4 6.7 %collective-permute-start.5 = (bf16[3584,256]{1,0:T(8,128)(2,1)S(1)}, bf16[3584,256]{1,0:T(8,128)(2,1)S(1)}, u32[]{:S(2)}, u32[]{:S(2)}) collective-permute-start(bf16[3584,256]{1,0:T(8,128)(2,1)S(1)} %convolution_convert_fusion), channel_id=1, source_target_pairs={{0,32},{32,0},{1,33},{33,1},{2,34},{34,2},{3,35},{35,3},{4,36},{36... | collective-permute-start | bytes 5505032 | tf_op jit(solution)/shard_map/ppermute | solution.py:70
  121.7 6.4 %collective-permute-start.6 = (bf16[256,3584]{1,0:T(8,128)(2,1)S(1)}, bf16[256,3584]{1,0:T(8,128)(2,1)S(1)}, u32[]{:S(2)}, u32[]{:S(2)}) collective-permute-start(bf16[256,3584]{1,0:T(8,128)(2,1)S(1)} %convolution_convert_fusion.1), channel_id=1, source_target_pairs={{0,32},{32,0},{1,33},{33,1},{2,34},{34,2},{3,35},{35,3},{4,36},{36... | collective-permute-start | bytes 5505032 | tf_op jit(solution)/shard_map/ppermute | solution.py:70
  125.1 6.1 %copy-start.1 = (bf16[448,3584]{1,0:T(8,128)(2,1)S(1)}, bf16[448,3584]{1,0:T(8,128)(2,1)}, u32[]{:S(2)}) copy-start(bf16[448,3584]{1,0:T(8,128)(2,1)} %param.13) | copy-start | bytes 9633796

commit v2 on v1

--- a/solution.py
+++ b/solution.py
@@ -54,7 +54,7 @@
 def groups_of_8(first):
     groups = {}
     for x, core, z, y in devices():
-        line, across = (z, x) if core == 0 else (x, z)
+        line, across = (x, z) if core == 0 else (z, x)
         turned = (y + 1 - core) % 4
         group, place = (across, turned // 2), (line, min(turned, 3 - turned))
         key, order = (group, place) if first else (place, group)
@@ -90,8 +90,7 @@
     far_resid = far_rows(resid_stream)
     enc_2 = jnp.concatenate([w_enc, other_core(w_enc)], axis=1)
     dec_2 = jnp.concatenate([w_dec, other_core(w_dec)], axis=0)
-    far_bias = other_core(b_enc)
-    bias_2 = jnp.concatenate([b_enc, far_bias], axis=0).astype(F32)
+    bias_2 = jnp.concatenate([b_enc, other_core(b_enc)], axis=0).astype(F32)
 
     scale = scale_of(resid_stream)
     far_scale = far_rows(scale)

time: 132 us -> 132 us (level)
  no operation moved by 1% of the time
where the time goes in v2:
time: 132 us; the launch traced here: 131 us
  blocking collectives  82.3 us (62%)
  matrix products  21.6 us (16%)
  other arithmetic  10.5 us (8%)
  starting transfers between devices  8.83 us (7%)
  waiting for transfers between devices  4.06 us (3%)
  local copies, waits for them, and re-layouts  3.3 us (2%)
    all_to_all x4, blocking collectives, exchange(): lax.all_to_all(values, ALL, 0, 0, axis_index_groups=groups_of_8(first), t...  82.3 us
    dot_general x6, matrix products, dot(): return jnp.dot(left, right, preferred_element_type=F32)  11.1 us
    dot_general x4, matrix products, contract_first(): lax.dot_general(left, right, (((0,), (0,)), ((), ())), preferred_element_...  8.39 us
    ppermute x5, starting transfers between devices, other_core(): return lax.ppermute(values, 'c', [(0, 1), (1, 0)])  5.63 us
    convert_element_type x2, other arithmetic, normed(): return (values.astype(F32) * scale * (1.0 + pre_gain)).astype(BF16)  5.24 us
    ppermute x5, waiting for transfers between devices, other_core(): return lax.ppermute(values, 'c', [(0, 1), (1, 0)])  3.33 us
    ppermute x2, starting transfers between devices, far_rows(): return lax.ppermute(values, ALL, pairs)  3.21 us
  transfers between devices with their start and end apart: 7, of which 2 were waited for; matrix products, arithmetic and copies ran while one was open for 16% of the time, Pallas kernels for 0%

profile of v2, /device:TPU:1, one launch (start us, length us, event | category | flops | bytes accessed | tf_op | source)
XLA Modules:
  0.0 131.5 jit_solution(9726902808160893888)
XLA Ops:
  0.6 1.5 %collective-permute-start.2 = (bf16[256]{0:T(256)(128)(2,1)}, bf16[256]{0:T(256)(128)(2,1)S(1)}, u32[]{:S(2)}, u32[]{:S(2)}) collective-permute-start(bf16[256]{0:T(256)(128)(2,1)} %param.15), channel_id=1, source_target_pairs={{0,32},{32,0},{1,33},{33,1},{2,34},{34,2},{3,35},{35,3},{4,36},{36... | collective-permute-start | bytes 1544 | tf_op jit(solution)/shard_map/ppermute | solution.py:70
  2.1 2.6 %collective-permute-start = (bf16[256,3584]{1,0:T(8,128)(2,1)}, bf16[256,3584]{1,0:T(8,128)(2,1)}, u32[]{:S(2)}, u32[]{:S(2)}) collective-permute-start(bf16[256,3584]{1,0:T(8,128)(2,1)} %param.9), channel_id=1, source_target_pairs={{0,64},{1,65},{2,66},{3,67},{4,68},{5,69},{6,70},{7,71},{8,72},{9,... | collective-permute-start | bytes 5505032 | tf_op jit(solution)/shard_map/ppermute | solution.py:51
  4.7 2.0 %fusion = f32[256]{0:T(256)S(1)} fusion(bf16[256,3584]{1,0:T(8,128)(2,1)} %param.9), kind=kLoop, calls=%fused_computation.5 | loop fusion | flops 2752256 | bytes 1836032 | tf_op jit(solution)/shard_map/reduce_sum | solution.py:19
  8.5 3.2 %fusion.2 = bf16[256,3584]{1,0:T(8,128)(2,1)} fusion(bf16[256,3584]{1,0:T(8,128)(2,1)} %param.9, f32[3584]{0:T(1024)S(1)} %broadcast_add_fusion, f32[256]{0:T(256)S(1)} %add_rsqrt_fusion), kind=kLoop, calls=%fused_computation.7 | loop fusion | flops 3670016 | bytes 3685376 | tf_op jit(solution)/shard_map/convert_element_type | solution.py:23
  11.8 3.6 %fusion.34 = f32[256,448]{0,1:T(8,128)S(1)} fusion(bf16[256,3584]{1,0:T(8,128)(2,1)} %fusion.2, bf16[3584,448]{0,1:T(8,128)(2,1)} %param.11), kind=kOutput, calls=%fused_computation.57 | convolution fusion | flops 822083584 | bytes 5505024 | tf_op jit(solution)/shard_map/dot_general | solution.py:27
  15.7 1.0 fusion.8
  17.4 2.1 %fusion.17 = f32[512,3584]{1,0:T(8,128)S(1)} fusion(bf16[448,3584]{1,0:T(8,128)(2,1)S(1)} %copy-done, bf16[256,448]{0,1:T(8,128)(2,1)S(1)} %fusion.8, pred[]{:T(512)S(6)} %eq.3), kind=kOutput, calls=%fused_computation.36 | convolution fusion | flops 1644396544 | bytes 10780673 | tf_op jit(solution)/shard_map/dot_general | solution.py:27
  19.6 1.8 %constant_dynamic-update-slice_fusion = bf16[3584,512]{1,0:T(8,128)(2,1)S(1)} fusion(bf16[3584,512]{1,0:T(8,128)(2,1)S(1)} %constant_dynamic-update-slice_fusion.1, bf16[3584,256]{1,0:T(8,128)(2,1)} %collective-permute-done.1), kind=kLoop, calls=%fused_computation.49 | loop fusion | bytes 3670016 | tf_op jit(solution)/shard_map/concatenate | solution.py:91
  21.6 1.7 %pad_maximum_fusion = bf16[512,3584]{1,0:T(8,128)(2,1)S(1)} fusion(bf16[256,3584]{1,0:T(8,128)(2,1)} %collective-permute-done.3, bf16[256,3584]{1,0:T(8,128)(2,1)S(1)} %copy-done.2), kind=kLoop, calls=%fused_computation.8 | loop fusion | flops 7340032 | bytes 7340032 | tf_op jit(solution)/shard_map/concatenate | solution.py:92
  23.3 1.1 fusion.7
  25.2 2.0 %multiply_convert_fusion = bf16[256,3584]{1,0:T(8,128)(2,1)S(1)} fusion(bf16[256,3584]{1,0:T(8,128)(2,1)} %collective-permute-done, f32[256]{0:T(256)S(1)} %bitcast.30, f32[3584]{0:T(1024)S(1)} %broadcast_add_fusion), kind=kLoop, calls=%fused_computation.12 | loop fusion | flops 3670016 | bytes 3685376 | tf_op jit(solution)/shard_map/convert_element_type | solution.py:23
  27.2 1.1 fusion.6
  28.5 2.1 %subtract_convert_fusion = bf16[512,3584]{1,0:T(8,128)(2,1)S(1)} fusion(f32[512,3584]{1,0:T(8,128)S(1)} %fusion.17, bf16[512,512]{1,0:T(8,128)(2,1)S(1)} %multiply_convert_fusion.1, bf16[512,3584]{1,0:T(8,128)(2,1)S(1)} %pad_maximum_fusion), kind=kOutput, calls=%fused_computation | convolution fusion | flops 1882718208 | bytes 15204352 | tf_op jit(solution)/shard_map/dot_general | solution.py:27
  30.6 30.5 %all_to_all.20 = bf16[8,64,3584]{2,1,0:T(8,128)(2,1)S(1)} all-to-all(bf16[8,64,3584]{2,1,0:T(8,128)(2,1)S(1)} %bitcast.27), channel_id=1, replica_groups={{3,0,67,64,19,16,83,80},{2,1,66,65,18,17,82,81},{7,4,71,68,23,20,87,84}..., dimensions={0} | all-to-all | bytes 7340032 | tf_op jit(solution)/shard_map/all_to_all | solution.py:66
  61.6 13.6 %all_to_all.21 = bf16[8,8,3584]{2,1,0:T(8,128)(2,1)S(1)} all-to-all(bf16[8,8,3584]{2,1,0:T(8,128)(2,1)S(1)} %fusion.16), channel_id=1, replica_groups={{3,2,7,6,11,10,15,14},{0,1,4,5,8,9,12,13},{67,66,71,70,75,74,79,78},{64..., dimensions={0} | all-to-all | bytes 917504 | tf_op jit(solution)/shard_map/all_to_all | solution.py:66
  75.4 10.9 %all_to_all.22 = bf16[8,8,3584]{2,1,0:T(8,128)(2,1)S(1)} all-to-all(bf16[8,8,3584]{2,1,0:T(8,128)(2,1)S(1)} %broadcast_in_dim.9), channel_id=1, replica_groups={{3,2,7,6,11,10,15,14},{0,1,4,5,8,9,12,13},{67,66,71,70,75,74,79,78},{64..., dimensions={0} | all-to-all | bytes 917504 | tf_op jit(solution)/shard_map/all_to_all | solution.py:66
  86.6 27.2 %all_to_all.23 = bf16[8,64,3584]{2,1,0:T(8,128)(2,1)S(1)} all-to-all(bf16[8,64,3584]{2,1,0:T(8,128)(2,1)S(1)} %broadcast_in_dim.11), channel_id=1, replica_groups={{3,0,67,64,19,16,83,80},{2,1,66,65,18,17,82,81},{7,4,71,68,23,20,87,84}..., dimensions={0} | all-to-all | bytes 7340032 | tf_op jit(solution)/shard_map/all_to_all | solution.py:66
  113.8 1.2 convolution_convert_fusion.1
  114.9 2.1 %fusion.5 = bf16[512,512]{1,0:T(8,128)(2,1)S(1)} fusion(bf16[512,3584]{1,0:T(8,128)(2,1)S(1)} %bitcast.25, bf16[512,3584]{1,0:T(8,128)(2,1)S(1)} %pad_maximum_fusion, f32[256,512]{1,0:T(8,128)S(1)} %fusion.6, f32[256,512]{1,0:T(8,128)S(1)} %fusion.7, pred[]{:T(512)S(6)} %eq.3), kind=kOutput, calls=%fused_computation.16 | convolution fusion | flops 1880621056 | bytes 8912897 | tf_op jit(solution)/shard_map/dot_general | solution.py:35
  117.2 1.2 convolution_convert_fusion
  118.4 3.6 %collective-permute-start.5 = (bf16[3584,256]{1,0:T(8,128)(2,1)S(1)}, bf16[3584,256]{1,0:T(8,128)(2,1)S(1)}, u32[]{:S(2)}, u32[]{:S(2)}) collective-permute-start(bf16[3584,256]{1,0:T(8,128)(2,1)S(1)} %convolution_convert_fusion), channel_id=1, source_target_pairs={{0,32},{32,0},{1,33},{33,1},{2,34},{34,2},{3,35},{35,3},{4,36},{36... | collective-permute-start | bytes 5505032 | tf_op jit(solution)/shard_map/ppermute | solution.py:70
  122.1 3.3 %collective-permute-done.5 = bf16[3584,256]{1,0:T(8,128)(2,1)S(1)} collective-permute-done((bf16[3584,256]{1,0:T(8,128)(2,1)S(1)}, bf16[3584,256]{1,0:T(8,128)(2,1)S(1)}, u32[]{:S(2)}, u32[]{:S(2)}) %collective-permute-start.5) | collective-permute-done | bytes 1835040 | tf_op jit(solution)/shard_map/ppermute | solution.py:70
  125.4 3.0 %add_multiply_fusion.1 = f32[3584,256]{1,0:T(8,128)} fusion(bf16[3584,256]{1,0:T(8,128)(2,1)S(1)} %collective-permute-done.5, bf16[256,3584]{1,0:T(8,128)(2,1)S(1)} %multiply_convert_fusion, bf16[256,3584]{1,0:T(8,128)(2,1)S(1)} %copy-done.4, bf16[512,512]{1,0:T(8,128)(2,1)S(1)} %maximum_select_fusion.1), kind=kOutput, calls=%fused_computation.11 | convolution fusion | flops 949616640 | bytes 9437184 | tf_op jit(solution)/shard_map/dot_general | solution.py:31
  128.4 3.0 %add_multiply_fusion = f32[256,3584]{1,0:T(8,128)} fusion(bf16[256,3584]{1,0:T(8,128)(2,1)S(1)} %collective-permute-done.6, bf16[512,3584]{1,0:T(8,128)(2,1)S(1)} %bitcast.26, bf16[512,512]{1,0:T(8,128)(2,1)S(1)} %multiply_convert_fusion.1), kind=kOutput, calls=%fused_computation.10 | convolution fusion | flops 942276608 | bytes 9437184 | tf_op jit(solution)/shard_map/dot_general | solution.py:31
  (37 shorter events, 5.1 us)
Async XLA Ops:
  0.6 16.8 %copy-start = (bf16[448,3584]{1,0:T(8,128)(2,1)S(1)}, bf16[448,3584]{1,0:T(8,128)(2,1)}, u32[]{:S(2)}) copy-start(bf16[448,3584]{1,0:T(8,128)(2,1)} %param.13) | copy-start | bytes 9633796
  0.6 18.9 %collective-permute-start.2 = (bf16[256]{0:T(256)(128)(2,1)}, bf16[256]{0:T(256)(128)(2,1)S(1)}, u32[]{:S(2)}, u32[]{:S(2)}) collective-permute-start(bf16[256]{0:T(256)(128)(2,1)} %param.15), channel_id=1, source_target_pairs={{0,32},{32,0},{1,33},{33,1},{2,34},{34,2},{3,35},{35,3},{4,36},{36... | collective-permute-start | bytes 1544 | tf_op jit(solution)/shard_map/ppermute | solution.py:70
  2.1 23.1 %collective-permute-start = (bf16[256,3584]{1,0:T(8,128)(2,1)}, bf16[256,3584]{1,0:T(8,128)(2,1)}, u32[]{:S(2)}, u32[]{:S(2)}) collective-permute-start(bf16[256,3584]{1,0:T(8,128)(2,1)} %param.9), channel_id=1, source_target_pairs={{0,64},{1,65},{2,66},{3,67},{4,68},{5,69},{6,70},{7,71},{8,72},{9,... | collective-permute-start | bytes 5505032 | tf_op jit(solution)/shard_map/ppermute | solution.py:51
  6.7 18.5 %collective-permute-start.4 = (f32[256,1]{0,1:T(1,128)S(1)}, f32[256,1]{0,1:T(1,128)S(1)}, u32[]{:S(2)}, u32[]{:S(2)}) collective-permute-start(f32[256,1]{0,1:T(1,128)S(1)} %bitcast.29), channel_id=1, source_target_pairs={{0,64},{1,65},{2,66},{3,67},{4,68},{5,69},{6,70},{7,71},{8,72},{9,... | collective-permute-start | bytes 3080 | tf_op jit(solution)/shard_map/ppermute | solution.py:51
  7.3 12.3 %collective-permute-start.1 = (bf16[3584,256]{1,0:T(8,128)(2,1)}, bf16[3584,256]{1,0:T(8,128)(2,1)}, u32[]{:S(2)}, u32[]{:S(2)}) collective-permute-start(bf16[3584,256]{1,0:T(8,128)(2,1)} %param.14), channel_id=1, source_target_pairs={{0,32},{32,0},{1,33},{33,1},{2,34},{34,2},{3,35},{35,3},{4,36},{36... | collective-permute-start | bytes 5505032 | tf_op jit(solution)/shard_map/ppermute | solution.py:70
  7.3 14.0 %collective-permute-start.3 = (bf16[256,3584]{1,0:T(8,128)(2,1)}, bf16[256,3584]{1,0:T(8,128)(2,1)}, u32[]{:S(2)}, u32[]{:S(2)}) collective-permute-start(bf16[256,3584]{1,0:T(8,128)(2,1)} %param.16), channel_id=1, source_target_pairs={{0,32},{32,0},{1,33},{33,1},{2,34},{34,2},{3,35},{35,3},{4,36},{36... | collective-permute-start | bytes 5505032 | tf_op jit(solution)/shard_map/ppermute | solution.py:70
  11.8 3.6 %copy-start.4 = (bf16[256,3584]{1,0:T(8,128)(2,1)S(1)}, bf16[256,3584]{1,0:T(8,128)(2,1)}, u32[]{:S(2)}) copy-start(bf16[256,3584]{1,0:T(8,128)(2,1)} %fusion.2) | copy-start | bytes 5505028
  11.8 4.0 %copy-start.7 = (bf16[3584,448]{0,1:T(8,128)(2,1)S(1)}, bf16[3584,448]{0,1:T(8,128)(2,1)}, u32[]{:S(2)}) copy-start(bf16[3584,448]{0,1:T(8,128)(2,1)} %param.12) | copy-start | bytes 9633796
  15.7 1.5 %copy-start.3 = (bf16[3584,256]{1,0:T(8,128)(2,1)S(1)}, bf16[3584,256]{1,0:T(8,128)(2,1)}, u32[]{:S(2)}) copy-start(bf16[3584,256]{1,0:T(8,128)(2,1)} %param.14) | copy-start | bytes 5505028
  17.4 2.2 %copy-start.6 = (bf16[256]{0:T(256)(128)(2,1)S(1)}, bf16[256]{0:T(256)(128)(2,1)}, u32[]{:S(2)}) copy-start(bf16[256]{0:T(256)(128)(2,1)} %param.15) | copy-start | bytes 1540
  19.5 2.1 %copy-start.2 = (bf16[256,3584]{1,0:T(8,128)(2,1)S(1)}, bf16[256,3584]{1,0:T(8,128)(2,1)}, u32[]{:S(2)}) copy-start(bf16[256,3584]{1,0:T(8,128)(2,1)} %param.16) | copy-start | bytes 5505028
  61.1 14.1 %copy-start.5 = (f32[3584]{0:T(1024)S(1)}, f32[3584]{0:T(1024)}, u32[]{:S(2)}) copy-start(f32[3584]{0:T(1024)} %param.17) | copy-start | bytes 43012
  118.4 7.0 %collective-permute-start.5 = (bf16[3584,256]{1,0:T(8,128)(2,1)S(1)}, bf16[3584,256]{1,0:T(8,128)(2,1)S(1)}, u32[]{:S(2)}, u32[]{:S(2)}) collective-permute-start(bf16[3584,256]{1,0:T(8,128)(2,1)S(1)} %convolution_convert_fusion), channel_id=1, source_target_pairs={{0,32},{32,0},{1,33},{33,1},{2,34},{34,2},{3,35},{35,3},{4,36},{36... | collective-permute-start | bytes 5505032 | tf_op jit(solution)/shard_map/ppermute | solution.py:70
  122.0 6.4 %collective-permute-start.6 = (bf16[256,3584]{1,0:T(8,128)(2,1)S(1)}, bf16[256,3584]{1,0:T(8,128)(2,1)S(1)}, u32[]{:S(2)}, u32[]{:S(2)}) collective-permute-start(bf16[256,3584]{1,0:T(8,128)(2,1)S(1)} %convolution_convert_fusion.1), channel_id=1, source_target_pairs={{0,32},{32,0},{1,33},{33,1},{2,34},{34,2},{3,35},{35,3},{4,36},{36... | collective-permute-start | bytes 5505032 | tf_op jit(solution)/shard_map/ppermute | solution.py:70
  125.4 6.1 %copy-start.1 = (bf16[448,3584]{1,0:T(8,128)(2,1)S(1)}, bf16[448,3584]{1,0:T(8,128)(2,1)}, u32[]{:S(2)}) copy-start(bf16[448,3584]{1,0:T(8,128)(2,1)} %param.13) | copy-start | bytes 9633796
